TPU v7x, 32 devices: a whole 2x2x4 slice. The times are simulated.
32 devices in a mesh: row: 8 (over z, core), col: 4 (over y, x).
Axes of the slice: x: 2, y: 2, z: 4, core: 2. Of those that a mesh axis runs over, the one named last changes fastest.
Arguments:
- grad: bfloat16 [2, 6144, 24576], P(None, 'row', 'col'), may hold values from -45 to 45, as said below
- memory: float32 [2, 6144, 24576], P(None, 'row', 'col'), may hold values from -6 to 6
- p_prev: float32 [2, 6144, 32], P(None, ('row', 'col')), may hold values from -6 to 6
- q_prev: float32 [2, 24576, 32], P(None, ('col', 'row')), may hold values from -1 to 1
Outputs:
- p_new: float32 [2, 6144, 32], P(None, ('row', 'col'))
- q_new: float32 [2, 24576, 32], P(None, ('col', 'row'))
- error: float32 [2, 6144, 24576], P(None, 'row', 'col')
Inputs may be any that keep to these rules, and one draw needn't show every extreme that they name: `grad`: real-valued gradient entries.
All inputs are finite; a program needn't handle non-finite values.
Results may differ from a plain program's by a relative error of at most 0.0003.
Values sent between devices are 32-bit elements; how exact they have to be, the bound alone decides.
A program may use at most 192 MiB of HBM per device.

v0:
```python
import jax
import jax.numpy as jnp
from jax import lax
from jax.sharding import PartitionSpec as P


def shards(grad, memory, p_prev, q_prev):
    highest = lax.Precision.HIGHEST
    left_rows = lax.all_gather(p_prev, "col", axis=1, tiled=True)
    right_rows = lax.all_gather(q_prev, "row", axis=1, tiled=True)
    approx = jnp.einsum("lrk,lck->lrc", left_rows, right_rows, precision=highest)
    merged = grad.astype(jnp.float32) + memory - approx
    partial_value = jnp.einsum("lrc,lck->lrk", merged, right_rows, precision=highest)
    left = lax.psum(partial_value, "col")
    gram_part = jnp.einsum("lrk,lrj->lkj", left, left, precision=highest)
    gram = lax.psum(gram_part, "row")
    factor = jnp.linalg.cholesky(gram)
    p_hat = lax.linalg.triangular_solve(factor, left, left_side=False, lower=True, transpose_a=True)
    right_part = jnp.einsum("lrc,lrk->lck", merged, p_hat, precision=highest)
    share_rows = right_part.shape[1] // lax.axis_size("row")
    right_full = lax.psum(right_part, "row")
    q_new = lax.dynamic_slice_in_dim(right_full, lax.axis_index("row") * share_rows, share_rows, 1)
    error = merged - jnp.einsum("lrk,lck->lrc", p_hat, right_full, precision=highest)
    left_share = p_hat.shape[1] // lax.axis_size("col")
    p_new = lax.dynamic_slice_in_dim(p_hat, lax.axis_index("col") * left_share, left_share, 1)
    return (p_new, q_new, error)


def solution(mesh):
    placed = (
        P(None, "row", "col"),
        P(None, "row", "col"),
        P(None, ("row", "col"), None),
        P(None, ("col", "row"), None),
    )
    return jax.shard_map(
        shards,
        mesh=mesh,
        in_specs=placed,
        out_specs=(
            P(None, ("row", "col"), None),
            P(None, ("col", "row"), None),
            P(None, "row", "col"),
        ),
        check_vma=False,
    )
```

profile of v0, /device:TPU:0, one launch (start us, length us, event | category | flops | bytes accessed | tf_op | source)
XLA Modules:
  0.0 335.4 jit_solution(1339748341165155115)
XLA Ops:
  7.2 0.0 all-gather.2.cloned.1.call-start
  7.2 0.7 all-gather.2.cloned.1.call-update
  7.9 0.0 all-reduce.3.cloned.1.call-start
  7.9 1.0 copy.15
  8.9 12.7 %all_gather.6 = f32[2,768,32]{2,0,1:T(2,128)S(1)} all-gather(f32[2,192,32]{2,0,1:T(2,128)S(1)} %copy.15), channel_id=1, replica_groups=mesh['row'=8,'col'=4] {'col'}, dimensions={1}, use_global_device_ids=true | all-gather | bytes 245760 | tf_op jit(solution)/shard_map/all_gather | solution.py:9
  21.6 16.0 %all-gather.2.cloned.1.call-done = f32[2,6144,32]{1,2,0:T(8,128)} async-done(((f32[2,768,32]{1,2,0:T(8,128)}), f32[2,6144,32]{1,2,0:T(8,128)}) %all-gather.2.cloned.1.call-update) | async-done | bytes 1572880 | tf_op jit(solution)/shard_map/all_gather | solution.py:10
  37.6 44.0 %add_subtract_fusion = f32[2,768,6144]{2,1,0:T(8,128)} fusion(f32[2,768,6144]{2,1,0:T(8,128)} %param.5, bf16[2,768,6144]{2,1,0:T(8,128)(2,1)} %param.4, f32[2,6144,32]{1,2,0:T(8,128)} %all-gather.2.cloned.1.call-done, f32[2,768,32]{2,0,1:T(2,128)S(1)} %all_gather.6), kind=kOutput, calls=%fused_computation | convolution fusion | flops 3652190208 | bytes 96141312 | tf_op jit(solution)/shard_map/lrk,lck->lrc/dot_general | solution.py:11
  81.6 39.0 %fusion.4 = f32[2,768,32]{1,2,0:T(8,128)} fusion(f32[2,768,6144]{2,1,0:T(8,128)} %add_subtract_fusion, f32[2,6144,32]{1,2,0:T(8,128)S(1)} %copy-done), kind=kOutput, calls=%fused_computation.14 | convolution fusion | flops 3623878656 | bytes 39518208 | tf_op jit(solution)/shard_map/lrc,lck->lrk/dot_general | solution.py:13
  120.5 0.0 all-reduce.3.cloned.1.call-update
  120.6 0.0 all-reduce.5.cloned.1.call-start
  120.6 41.8 %all-reduce.3.cloned.1.call-done = f32[2,768,32]{1,2,0:T(8,128)} async-done(((f32[2,768,32]{1,2,0:T(8,128)}), f32[2,768,32]{1,2,0:T(8,128)}) %all-reduce.3.cloned.1.call-update) | async-done | bytes 196624 | tf_op jit(solution)/shard_map/psum | solution.py:14
  162.4 1.3 fusion.5
  163.8 28.1 %psum.22 = f32[2,32,32]{1,2,0:T(8,128)S(1)} all-reduce(f32[2,32,32]{1,2,0:T(8,128)S(1)} %fusion.5), channel_id=1, replica_groups=mesh['row'=8,'col'=4] {'row'}, use_global_device_ids=true, to_apply=%region_1.0 | all-reduce | flops 2048 | bytes 16384 | tf_op jit(solution)/shard_map/psum | solution.py:16
  191.9 0.1 copy.18
  192.0 5.9 %custom-call.7 = f32[2,32,32]{2,1,0:T(8,128)S(1)} custom-call(f32[2,32,32]{2,1,0:T(8,128)S(1)} %fusion.3), custom_call_target="Cholesky" | custom-call | tf_op jit(solution)/shard_map/jit(cholesky)/cholesky | solution.py:17
  197.9 0.1 compare_reduce_fusion
  198.0 0.1 select_bitcast_fusion
  198.1 4.9 %custom-call.8 = f32[2,1,32,32]{2,3,1,0:T(8,128)S(1)} custom-call(f32[2,1,32,32]{3,2,1,0:T(8,128)S(1)} %select_bitcast_fusion), custom_call_target="InvertDiagBlocksLowerTriangular" | custom-call | tf_op jit(solution)/shard_map/triangular_solve | solution.py:18
  203.0 1.3 fusion.1
  204.3 26.9 %fusion.6 = f32[2,6144,32]{1,2,0:T(8,128)} fusion(f32[2,768,6144]{2,1,0:T(8,128)} %add_subtract_fusion, f32[2,768,32]{1,2,0:T(8,128)S(1)} %fusion.1), kind=kOutput, calls=%fused_computation.16 | convolution fusion | flops 3623878656 | bytes 39518208 | tf_op jit(solution)/shard_map/lrc,lrk->lck/dot_general | solution.py:19
  231.2 0.7 constant_dynamic-slice_fusion.1
  231.9 58.6 %all-reduce.5.cloned.1.call-done = f32[2,6144,32]{1,2,0:T(8,128)} async-done(((f32[2,6144,32]{1,2,0:T(8,128)}), f32[2,6144,32]{1,2,0:T(8,128)}) %all-reduce.5.cloned.1.call-update) | async-done | bytes 1572880 | tf_op jit(solution)/shard_map/psum | solution.py:21
  290.5 36.7 %convolution_subtract_fusion = f32[2,768,6144]{2,1,0:T(8,128)} fusion(f32[2,768,6144]{2,1,0:T(8,128)} %add_subtract_fusion, f32[2,768,32]{1,2,0:T(8,128)S(1)} %fusion.1, f32[2,6144,32]{1,2,0:T(8,128)} %all-reduce.5.cloned.1.call-done), kind=kOutput, calls=%fused_computation.1 | convolution fusion | flops 3633315840 | bytes 77266944 | tf_op jit(solution)/shard_map/lrk,lck->lrc/dot_general | solution.py:23
  327.2 1.6 constant_dynamic-slice_fusion
  (7 shorter events, 0.1 us)
Async XLA Ops:
  7.2 30.4 %all-gather.2.cloned.1.call-start = ((), (), s32[]{:S(2)}) async-start(), calls=%async_computation | async-start | bytes 1769472 | tf_op jit(solution)/shard_map/all_gather | solution.py:10
  7.9 154.5 %all-reduce.3.cloned.1.call-start = ((), (), s32[]{:S(2)}) async-start(), calls=%async_computation.1 | async-start | bytes 393216 | tf_op jit(solution)/shard_map/psum | solution.py:14
  37.6 44.0 %copy-start = (f32[2,6144,32]{1,2,0:T(8,128)S(1)}, f32[2,6144,32]{1,2,0:T(8,128)}, u32[]{:S(2)}) copy-start(f32[2,6144,32]{1,2,0:T(8,128)} %all-gather.2.cloned.1.call-done) | copy-start | bytes 4718596
  120.6 169.9 %all-reduce.5.cloned.1.call-start = ((), (), s32[]{:S(2)}) async-start(), calls=%async_computation.2 | async-start | bytes 3145728 | tf_op jit(solution)/shard_map/psum | solution.py:21
Sparse Core Ops, SparseCore 0:
  9.6 27.9 all-gather.1
  120.7 41.7 all-reduce.2
  231.3 59.1 all-reduce.4
where the time goes:
time: 336 us; the launch traced here: 335 us
  matrix products  149 us (44%)
  waiting for transfers between devices  117 us (35%)
  blocking collectives  40.8 us (12%)
  between operations  13.8 us (4%)
  other arithmetic  11 us (3%)
  local copies, waits for them, and re-layouts  3.39 us (1%)
    psum x1, waiting for transfers between devices, shards(): right_full = lax.psum(right_part, 'row')  58.6 us
    dot_general x1, matrix products, shards(): jnp.einsum('lrk,lck->lrc', left_rows, right_rows, precision=highest)  44 us
    psum x1, waiting for transfers between devices, shards(): left = lax.psum(partial_value, 'col')  41.8 us
    dot_general x1, matrix products, shards(): jnp.einsum('lrc,lck->lrk', merged, right_rows, precision=highest)  39 us
    dot_general x1, matrix products, shards(): jnp.einsum('lrk,lck->lrc', p_hat, right_full, precision=highest)  36.7 us
    psum x1, blocking collectives, shards(): gram = lax.psum(gram_part, 'row')  28.1 us
    dot_general x1, matrix products, shards(): right_part = jnp.einsum('lrc,lrk->lck', merged, p_hat, precision=highest)  26.9 us
    all_gather x1, waiting for transfers between devices, shards(): right_rows = lax.all_gather(q_prev, 'row', axis=1, tiled=True)  16 us
  transfers between devices with their start and end apart: 3, of which 3 were waited for; matrix products, arithmetic and copies ran while one was open for 1% of the time, Pallas kernels for 0%

commit v1 on v0

--- a/solution.py
+++ b/solution.py
@@ -13,7 +13,7 @@
     partial_value = jnp.einsum("lrc,lck->lrk", merged, right_rows, precision=highest)
     left = lax.psum(partial_value, "col")
     gram_part = jnp.einsum("lrk,lrj->lkj", left, left, precision=highest)
-    gram = lax.psum(gram_part, "row")
+    gram = jnp.sum(lax.all_gather(gram_part, "row"), axis=0)
     factor = jnp.linalg.cholesky(gram)
     p_hat = lax.linalg.triangular_solve(factor, left, left_side=False, lower=True, transpose_a=True)
     right_part = jnp.einsum("lrc,lrk->lck", merged, p_hat, precision=highest)

time: 336 us -> 325 us (0.967)
  blocking collectives: 40.8 us -> 26.9 us
    psum x1 -> x0, blocking collectives: 28.1 us -> none  [shards(): gram = lax.psum(gram_part, 'row')]
    all_gather x0 -> x1, blocking collectives: none -> 14.3 us  [shards(): gram = jnp.sum(lax.all_gather(gram_part, 'row'), axis=0)]
where the time goes in v1:
time: 325 us; the launch traced here: 324 us
  matrix products  149 us (46%)
  waiting for transfers between devices  120 us (37%)
  blocking collectives  26.9 us (8%)
  between operations  13.8 us (4%)
  other arithmetic  11.3 us (3%)
  local copies, waits for them, and re-layouts  3.39 us (1%)
    psum x1, waiting for transfers between devices, shards(): right_full = lax.psum(right_part, 'row')  61.3 us
    dot_general x1, matrix products, shards(): jnp.einsum('lrk,lck->lrc', left_rows, right_rows, precision=highest)  44 us
    psum x1, waiting for transfers between devices, shards(): left = lax.psum(partial_value, 'col')  41.8 us
    dot_general x1, matrix products, shards(): jnp.einsum('lrc,lck->lrk', merged, right_rows, precision=highest)  39 us
    dot_general x1, matrix products, shards(): jnp.einsum('lrk,lck->lrc', p_hat, right_full, precision=highest)  36.7 us
    dot_general x1, matrix products, shards(): right_part = jnp.einsum('lrc,lrk->lck', merged, p_hat, precision=highest)  26.9 us
    all_gather x1, waiting for transfers between devices, shards(): right_rows = lax.all_gather(q_prev, 'row', axis=1, tiled=True)  16 us
    all_gather x1, blocking collectives, shards(): gram = jnp.sum(lax.all_gather(gram_part, 'row'), axis=0)  14.3 us
  transfers between devices with their start and end apart: 3, of which 3 were waited for; matrix products, arithmetic and copies ran while one was open for 1% of the time, Pallas kernels for 0%

profile of v1, /device:TPU:0, one launch (start us, length us, event | category | flops | bytes accessed | tf_op | source)
XLA Modules:
  0.0 324.5 jit_solution(15090341324582823974)
XLA Ops:
  7.2 0.0 all-gather.3.cloned.1.call-start
  7.2 0.7 all-gather.3.cloned.1.call-update
  7.9 0.0 all-reduce.3.cloned.1.call-start
  7.9 1.0 copy.13
  8.9 12.7 %all_gather.12 = f32[2,768,32]{2,0,1:T(2,128)S(1)} all-gather(f32[2,192,32]{2,0,1:T(2,128)S(1)} %copy.13), channel_id=1, replica_groups=mesh['row'=8,'col'=4] {'col'}, dimensions={1}, use_global_device_ids=true | all-gather | bytes 245760 | tf_op jit(solution)/shard_map/all_gather | solution.py:9
  21.6 16.0 %all-gather.3.cloned.1.call-done = f32[2,6144,32]{1,2,0:T(8,128)} async-done(((f32[2,768,32]{1,2,0:T(8,128)}), f32[2,6144,32]{1,2,0:T(8,128)}) %all-gather.3.cloned.1.call-update) | async-done | bytes 1572880 | tf_op jit(solution)/shard_map/all_gather | solution.py:10
  37.6 44.0 %add_subtract_fusion = f32[2,768,6144]{2,1,0:T(8,128)} fusion(f32[2,768,6144]{2,1,0:T(8,128)} %param.5, bf16[2,768,6144]{2,1,0:T(8,128)(2,1)} %param.4, f32[2,6144,32]{1,2,0:T(8,128)} %all-gather.3.cloned.1.call-done, f32[2,768,32]{2,0,1:T(2,128)S(1)} %all_gather.12), kind=kOutput, calls=%fused_computation | convolution fusion | flops 3652190208 | bytes 96141312 | tf_op jit(solution)/shard_map/lrk,lck->lrc/dot_general | solution.py:11
  81.6 39.0 %fusion.4 = f32[2,768,32]{1,2,0:T(8,128)} fusion(f32[2,768,6144]{2,1,0:T(8,128)} %add_subtract_fusion, f32[2,6144,32]{1,2,0:T(8,128)S(1)} %copy-done), kind=kOutput, calls=%fused_computation.14 | convolution fusion | flops 3623878656 | bytes 39518208 | tf_op jit(solution)/shard_map/lrc,lck->lrk/dot_general | solution.py:13
  120.5 0.0 all-reduce.3.cloned.1.call-update
  120.6 0.0 all-reduce.5.cloned.1.call-start
  120.6 41.8 %all-reduce.3.cloned.1.call-done = f32[2,768,32]{1,2,0:T(8,128)} async-done(((f32[2,768,32]{1,2,0:T(8,128)}), f32[2,768,32]{1,2,0:T(8,128)}) %all-reduce.3.cloned.1.call-update) | async-done | bytes 196624 | tf_op jit(solution)/shard_map/psum | solution.py:14
  162.4 1.3 fusion.5
  163.8 14.3 %all-gather = f32[16,32,32]{2,1,0:T(8,128)S(1)} all-gather(f32[2,32,32]{2,1,0:T(8,128)S(1)} %fusion.5), channel_id=2, replica_groups=mesh['row'=8,'col'=4] {'row'}, dimensions={0}, use_global_device_ids=true | all-gather | bytes 73728 | tf_op jit(solution)/shard_map/all_gather | solution.py:16
  178.0 0.1 copy.15
  178.1 6.1 %custom-call.7 = f32[2,32,32]{2,1,0:T(8,128)S(1)} custom-call(f32[2,32,32]{2,1,0:T(8,128)S(1)} %fusion.3), custom_call_target="Cholesky" | custom-call | tf_op jit(solution)/shard_map/jit(cholesky)/cholesky | solution.py:17
  184.3 0.1 compare_reduce_fusion
  184.4 0.1 select_bitcast_fusion
  184.5 4.9 %custom-call.8 = f32[2,1,32,32]{2,3,1,0:T(8,128)S(1)} custom-call(f32[2,1,32,32]{3,2,1,0:T(8,128)S(1)} %select_bitcast_fusion), custom_call_target="InvertDiagBlocksLowerTriangular" | custom-call | tf_op jit(solution)/shard_map/triangular_solve | solution.py:18
  189.4 1.3 fusion.1
  190.7 26.9 %fusion.6 = f32[2,6144,32]{1,2,0:T(8,128)} fusion(f32[2,768,6144]{2,1,0:T(8,128)} %add_subtract_fusion, f32[2,768,32]{1,2,0:T(8,128)S(1)} %fusion.1), kind=kOutput, calls=%fused_computation.16 | convolution fusion | flops 3623878656 | bytes 39518208 | tf_op jit(solution)/shard_map/lrc,lrk->lck/dot_general | solution.py:19
  217.6 0.7 constant_dynamic-slice_fusion.1
  218.3 61.3 %all-reduce.5.cloned.1.call-done = f32[2,6144,32]{1,2,0:T(8,128)} async-done(((f32[2,6144,32]{1,2,0:T(8,128)}), f32[2,6144,32]{1,2,0:T(8,128)}) %all-reduce.5.cloned.1.call-update) | async-done | bytes 1572880 | tf_op jit(solution)/shard_map/psum | solution.py:21
  279.6 36.7 %convolution_subtract_fusion = f32[2,768,6144]{2,1,0:T(8,128)} fusion(f32[2,768,6144]{2,1,0:T(8,128)} %add_subtract_fusion, f32[2,768,32]{1,2,0:T(8,128)S(1)} %fusion.1, f32[2,6144,32]{1,2,0:T(8,128)} %all-reduce.5.cloned.1.call-done), kind=kOutput, calls=%fused_computation.1 | convolution fusion | flops 3633315840 | bytes 77266944 | tf_op jit(solution)/shard_map/lrk,lck->lrc/dot_general | solution.py:23
  316.3 1.6 constant_dynamic-slice_fusion
  (8 shorter events, 0.1 us)
Async XLA Ops:
  7.2 30.4 %all-gather.3.cloned.1.call-start = ((), (), s32[]{:S(2)}) async-start(), calls=%async_computation | async-start | bytes 1769472 | tf_op jit(solution)/shard_map/all_gather | solution.py:10
  7.9 154.5 %all-reduce.3.cloned.1.call-start = ((), (), s32[]{:S(2)}) async-start(), calls=%async_computation.1 | async-start | bytes 393216 | tf_op jit(solution)/shard_map/psum | solution.py:14
  37.6 44.0 %copy-start = (f32[2,6144,32]{1,2,0:T(8,128)S(1)}, f32[2,6144,32]{1,2,0:T(8,128)}, u32[]{:S(2)}) copy-start(f32[2,6144,32]{1,2,0:T(8,128)} %all-gather.3.cloned.1.call-done) | copy-start | bytes 4718596
  120.6 159.0 %all-reduce.5.cloned.1.call-start = ((), (), s32[]{:S(2)}) async-start(), calls=%async_computation.2 | async-start | bytes 3145728 | tf_op jit(solution)/shard_map/psum | solution.py:21
Sparse Core Ops, SparseCore 0:
  9.6 27.9 all-gather.2
  120.7 41.7 all-reduce.2
  217.7 61.8 all-reduce.4
